TPU v7x, 32 devices: a whole 2x2x4 slice. The times are simulated.
32 devices in a mesh: lat: 4 (over y, x), lev: 8 (over z, core).
Axes of the slice: x: 2, y: 2, z: 4, core: 2. Of those that a mesh axis runs over, the one named last changes fastest.
Arguments:
- tracers: float32 [2, 128, 64, 128], P(None, 'lev', 'lat'), may hold values from -6 to 6
- layer_mass: float32 [128, 64, 128], P('lev', 'lat'), may hold values from 0.5 to 2
- courant: float32 [128, 64], P('lev', 'lat'), may hold values from 0.1 to 0.9
- remap: float32 [128, 128], replicated, may hold values from 0 to 1, as said below
- cost_class: int32 [64, 128], P('lat', 'lev'), may hold values from 0 to 2
- spans: int32 [512, 1], P(('lat', 'lev')), may hold values from 0 to 3; in each aligned block of 16 rows (0 to 15, 16 to 31, ...) at most 4 rows name the same one
- w_up: bfloat16 [4, 256, 512], P('lat'), may hold values from -0.375 to 0.375
- b_up: float32 [4, 512], P('lat'), may hold values from -6 to 6
- w_mid: bfloat16 [4, 512, 512], P('lat'), may hold values from -0.25 to 0.25
- w_down: bfloat16 [4, 512, 256], P('lat'), may hold values from -0.25 to 0.25
- sw_up: bfloat16 [4, 256, 512], P('lat'), may hold values from -0.375 to 0.375
- sw_down: bfloat16 [4, 512, 256], P('lat'), may hold values from -0.25 to 0.25
Outputs:
- tracers_out: float32 [2, 128, 64, 128], P(None, None, 'lat', 'lev')
Inputs may be any that keep to these rules, and one draw needn't show every extreme that they name: `remap`: diagonal entries are 1, the others lie between 0 and 1 / 128. `spans`: among the 16 rows of one device (aligned blocks of 16 rows, in the order of the devices along lat then lev), no value appears more than 4 times, and one value appears exactly 4 times.
All inputs are finite; a program needn't handle non-finite values.
Results may differ from a plain program's by a relative error of at most 0.005.
Values may be sent and summed in bfloat16 or wider, within the bound.
A program may use at most 64 MiB of HBM per device.

v0:
```python
import jax
import jax.numpy as jnp
from jax import lax
from jax.sharding import PartitionSpec as P

LEV = 128
SUBSTEPS = 4
BLK = 16


def minmod(first, second):
    return 0.5 * (jnp.sign(first) + jnp.sign(second)) * jnp.minimum(jnp.abs(first), jnp.abs(second))


def advect(fields, speeds):
    for substep in range(SUBSTEPS):
        east_cell = jnp.roll(fields, -1, axis=-1)
        west_cell = jnp.roll(fields, 1, axis=-1)
        slopes = minmod(east_cell - fields, fields - west_cell)
        fluxes = speeds * (fields + 0.5 * (1.0 - speeds) * slopes)
        fields = fields - (fluxes - jnp.roll(fluxes, 1, axis=-1))
    return fields


def remap_levels(remap, fields):
    masses = jnp.einsum("kl,flyx->fkyx", remap, fields, precision=lax.Precision.HIGHEST)
    return masses[1:] / masses[0]


def physics(features, layer_up, bias_up, layer_mid, layer_down, short_up, short_down):
    hidden = jax.nn.silu(
        jnp.dot(features, layer_up, preferred_element_type=jnp.float32) + bias_up
    ).astype(jnp.bfloat16)
    deeper = jax.nn.silu(jnp.dot(hidden, layer_mid, preferred_element_type=jnp.float32)).astype(
        jnp.bfloat16
    )
    main_out = jnp.dot(deeper, layer_down, preferred_element_type=jnp.float32)
    shortwave = jax.nn.silu(jnp.dot(features, short_up, preferred_element_type=jnp.float32)).astype(
        jnp.bfloat16
    )
    side_out = jnp.dot(shortwave, short_down, preferred_element_type=jnp.float32)
    return (main_out, side_out)


def shards(
    tracers,
    layer_mass,
    courant,
    remap,
    cost_class,
    spans,
    w_up,
    b_up,
    w_mid,
    w_down,
    sw_up,
    sw_down,
):
    fields = jnp.concatenate([layer_mass[None], tracers * layer_mass[None]], axis=0)
    fields = advect(fields, courant[None, :, :, None])
    regrouped = lax.all_to_all(fields, "lev", split_axis=3, concat_axis=1, tiled=True)
    mixing = remap_levels(remap, regrouped)
    width = mixing.shape[2] * mixing.shape[3]
    n_blocks = width // BLK
    groups = lax.axis_size("lat")
    most_blocks = max(2, (n_blocks + groups - 1) // groups)
    slots = groups * most_blocks
    features = mixing.reshape(2 * LEV, width).T.astype(jnp.bfloat16)
    column_blocks = features.reshape(n_blocks, BLK * 2 * LEV)
    factor = cost_class.astype(jnp.float32) * 0.5
    target = spans[:, 0]
    positions = jnp.arange(n_blocks, dtype=jnp.int32)
    earlier = positions[:, None] > positions[None, :]
    same_net = target[:, None] == target[None, :]
    slot_rank = jnp.sum((earlier & same_net).astype(jnp.int32), axis=1)
    slot_id = target * most_blocks + slot_rank
    placing = (jnp.arange(slots, dtype=jnp.int32)[:, None] == slot_id[None, :]).astype(jnp.float32)
    outgoing = jnp.dot(
        placing.astype(jnp.bfloat16), column_blocks, preferred_element_type=jnp.float32
    )
    outgoing = outgoing.astype(jnp.bfloat16).reshape(groups, most_blocks * BLK, 2 * LEV)
    sent_factor = (
        jnp.dot(placing, factor, precision=lax.Precision.HIGHEST)
        .astype(jnp.bfloat16)
        .reshape(groups, most_blocks * BLK)
    )
    incoming, incoming_factor = (
        lax.all_to_all(outgoing, "lat", split_axis=0, concat_axis=0, tiled=True),
        lax.all_to_all(sent_factor, "lat", split_axis=0, concat_axis=0, tiled=True),
    )
    main_out, side_out = physics(
        incoming.reshape(slots * BLK, 2 * LEV),
        w_up[0],
        b_up[0],
        w_mid[0],
        w_down[0],
        sw_up[0],
        sw_down[0],
    )
    owner_sum = (
        main_out + incoming_factor.reshape(slots * BLK).astype(jnp.float32)[:, None] * side_out
    ).astype(jnp.bfloat16)
    returned = lax.all_to_all(
        owner_sum.reshape(groups, most_blocks * BLK, 2 * LEV),
        "lat",
        split_axis=0,
        concat_axis=0,
        tiled=True,
    )
    tendency = jnp.dot(
        placing.T.astype(jnp.bfloat16),
        returned.reshape(slots, BLK * 2 * LEV),
        preferred_element_type=jnp.float32,
    )
    tendency = tendency.astype(jnp.bfloat16).reshape(width, 2 * LEV)
    update = tendency.astype(jnp.float32).T.reshape(mixing.shape)
    return mixing + update


def solution(mesh):
    placed = (
        P(None, "lev", "lat", None),
        P("lev", "lat", None),
        P("lev", "lat"),
        P(),
        P("lat", "lev"),
        P(("lat", "lev"), None),
        P("lat", None, None),
        P("lat", None),
        P("lat", None, None),
        P("lat", None, None),
        P("lat", None, None),
        P("lat", None, None),
    )
    return jax.shard_map(
        shards, mesh=mesh, in_specs=placed, out_specs=P(None, None, "lat", "lev"), check_vma=False
    )
```

profile of v0, /device:TPU:0, one launch (start us, length us, event | category | flops | bytes accessed | tf_op | source)
XLA Modules:
  0.0 70.7 jit_solution(11831857448592502894)
XLA Ops:
  0.0 1.1 %broadcast_multiply_fusion = f32[2,16,16,128]{3,2,1,0:T(8,128)S(1)} fusion(f32[2,16,16,128]{3,2,1,0:T(8,128)} %param.12, f32[16,16,128]{2,1,0:T(8,128)} %param.13), kind=kLoop, calls=%fused_computation.59 | loop fusion | flops 65536 | bytes 655360 | tf_op jit(solution)/shard_map/mul | solution.py:59
  1.1 1.1 %fusion.10 = (f32[3,16,16,127]{3,2,1,0:T(8,128)S(1)}, f32[3,16,16,127]{3,2,1,0:T(8,128)S(1)}) fusion(f32[2,16,16,128]{3,2,1,0:T(8,128)S(1)} %broadcast_multiply_fusion, f32[1,16,16,128]{3,2,1,0:T(8,128)} %bitcast.76), kind=kLoop, calls=%fused_computation.24 | loop fusion | flops 195072 | bytes 1173504 | tf_op jit(solution)/shard_map/concatenate | solution.py:59
  2.2 1.1 %fusion.11 = (f32[3,16,16,1]{3,2,1,0:T(8,128)S(1)}, f32[3,16,16,1]{3,2,1,0:T(8,128)S(1)}) fusion(f32[2,16,16,128]{3,2,1,0:T(8,128)S(1)} %broadcast_multiply_fusion, f32[1,16,16,128]{3,2,1,0:T(8,128)} %bitcast.77), kind=kLoop, calls=%fused_computation.25 | loop fusion | flops 1536 | bytes 399360 | tf_op jit(solution)/shard_map/concatenate | solution.py:59
  3.4 0.7 subtract_multiply_fusion
  4.1 1.4 %add_multiply_fusion.3 = f32[3,16,16,128]{3,2,1,0:T(8,128)S(1)} fusion(f32[3,16,16,127]{3,2,1,0:T(8,128)S(1)} %get-tuple-element.18, f32[3,16,16,1]{3,2,1,0:T(8,128)S(1)} %get-tuple-element.20, f32[3,16,16,1]{3,2,1,0:T(8,128)S(1)} %get-tuple-element.19, f32[3,16,16,127]{3,2,1,0:T(8,128)S(1)} %get-tuple-element.17, ...), kind=kLoop, calls=%fused_computation.47 | loop fusion | flops 1572864 | bytes 1574912 | tf_op jit(solution)/shard_map/mul | solution.py:20
  6.0 0.2 fusion.46
  6.2 0.5 add_multiply_fusion.2
  7.2 0.2 fusion.44
  7.4 0.5 add_multiply_fusion.1
  8.4 0.2 fusion.42
  8.6 0.5 add_multiply_fusion
  9.4 2.2 %copy.105 = f32[3,16,16,128]{2,1,0,3:T(8,128)} copy(f32[3,16,16,128]{3,2,1,0:T(8,128)S(1)} %fusion.17) | data formatting | bytes 786432 | tf_op jit(solution)/shard_map/sub | solution.py:21
  11.7 3.4 %reshape.75 = f32[8,1,12288]{2,1,0:T(1,128)} reshape(f32[128,3,16,16]{3,2,1,0:T(8,128)} %bitcast.69) | data formatting | bytes 786432
  15.1 6.4 %all-to-all-start = ((f32[8,1,12288]{2,1,0:T(1,128)}), f32[8,1,12288]{2,1,0:T(1,128)S(1)}, u32[]{:S(2)}, u32[]{:S(2)}) async-start(f32[8,1,12288]{2,1,0:T(1,128)} %reshape.75), calls=%async_computation | async-start | bytes 786432 | tf_op jit(solution)/shard_map/all_to_all | solution.py:61
  21.7 0.7 all_to_all.33
  22.4 11.5 %all-to-all-done = f32[8,1,12288]{2,1,0:T(1,128)S(1)} async-done(((f32[8,1,12288]{2,1,0:T(1,128)}), f32[8,1,12288]{2,1,0:T(1,128)S(1)}, u32[]{:S(2)}, u32[]{:S(2)}) %all-to-all-start) | async-done | bytes 393248 | tf_op jit(solution)/shard_map/all_to_all | solution.py:61
  33.9 3.7 %all-to-all-start.2 = ((bf16[4,1,64]{2,1,0:T(2,128)(2,1)}), bf16[4,1,64]{2,1,0:T(2,128)(2,1)S(1)}, u32[]{:S(2)}, u32[]{:S(2)}) async-start(bf16[4,1,64]{2,1,0:T(2,128)(2,1)} %all_to_all.33), calls=%async_computation.2 | async-start | bytes 4096 | tf_op jit(solution)/shard_map/all_to_all | solution.py:89
  37.7 0.5 broadcast.45
  38.2 1.6 %reduce.4 = f32[8,12288]{1,0:T(8,128)S(1)} reduce(f32[8,1,12288]{2,1,0:T(1,128)S(1)} %all-to-all-done, f32[]{:T(128)} %broadcast.45), dimensions={1}, to_apply=%all_to_all.25.reduce_sub_computation | reduce | bytes 786436 | tf_op jit(solution)/shard_map/all_to_all | solution.py:61
  39.8 2.7 %reshape.76 = f32[128,3,16,16]{3,2,1,0:T(8,128)} reshape(f32[8,12288]{1,0:T(8,128)S(1)} %reduce.4) | data formatting | bytes 786432
  42.5 4.9 %copy.106 = f32[3,16,16,8,16]{1,3,4,2,0:T(8,128)} copy(f32[3,16,16,8,16]{2,1,0,4,3:T(8,128)} %bitcast.70) | data formatting | bytes 786432 | tf_op jit(solution)/shard_map/all_to_all | solution.py:61
  47.3 2.5 %all_to_all.28 = f32[3,128,16,16]{1,3,2,0:T(8,128)S(1)} reshape(f32[3,8,16,16,16]{2,1,4,3,0:T(8,128)} %bitcast.71) | data formatting | bytes 786432 | tf_op jit(solution)/shard_map/all_to_all | solution.py:61
  49.8 0.5 convolution_bitcast_fusion
  50.8 0.7 %reshape.54 = bf16[4,64,256]{2,1,0:T(8,128)(2,1)} reshape(bf16[16,4096]{1,0:T(8,128)(2,1)S(1)} %convolution_convert_fusion.1) | data formatting | bytes 262144 | tf_op jit(solution)/shard_map/reshape | solution.py:81
  51.5 4.2 %all-to-all-start.1 = ((bf16[4,64,256]{2,1,0:T(8,128)(2,1)}), bf16[4,64,256]{2,1,0:T(8,128)(2,1)S(1)}, u32[]{:S(2)}, u32[]{:S(2)}) async-start(bf16[4,64,256]{2,1,0:T(8,128)(2,1)} %reshape.54), calls=%async_computation.1 | async-start | bytes 262144 | tf_op jit(solution)/shard_map/all_to_all | solution.py:88
  55.8 4.9 %all-to-all-done.1 = bf16[4,64,256]{2,1,0:T(8,128)(2,1)S(1)} async-done(((bf16[4,64,256]{2,1,0:T(8,128)(2,1)}), bf16[4,64,256]{2,1,0:T(8,128)(2,1)S(1)}, u32[]{:S(2)}, u32[]{:S(2)}) %all-to-all-start.1) | async-done | bytes 131104 | tf_op jit(solution)/shard_map/all_to_all | solution.py:88
  60.7 0.3 multiply_convert_fusion.2
  61.1 0.5 fusion.8
  61.6 0.4 fusion.2
  62.0 7.4 %all_to_all.38 = bf16[4,64,256]{2,1,0:T(8,128)(2,1)S(1)} all-to-all(bf16[4,64,256]{2,1,0:T(8,128)(2,1)S(1)} %bitcast.85), channel_id=1, replica_groups=mesh['lat'=4,'lev'=8] {'lat'}, dimensions={0} | all-to-all | bytes 262144 | tf_op jit(solution)/shard_map/all_to_all | solution.py:103
  69.5 0.2 fusion
  69.9 0.7 %copy_add_fusion = f32[2,128,16,16]{1,3,2,0:T(8,128)} fusion(f32[2,128,16,16]{1,0,3,2:T(2,128)S(1)} %reshape.62, f32[128,16,16]{0,2,1:T(8,128)S(1)} %slice_bitcast_fusion, f32[3,128,16,16]{1,3,2,0:T(8,128)S(1)} %convolution_bitcast_fusion), kind=kLoop, calls=%fused_computation.54 | loop fusion | flops 131072 | bytes 917504 | tf_op jit(solution)/shard_map/add | solution.py:117
  (48 shorter events, 3.0 us)
Async XLA Ops:
  0.0 61.0 %copy-start = (bf16[1,512,512]{2,1,0:T(8,128)(2,1)S(1)}, bf16[1,512,512]{2,1,0:T(8,128)(2,1)}, u32[]{:S(2)}) copy-start(bf16[1,512,512]{2,1,0:T(8,128)(2,1)} %param.20) | copy-start | bytes 1572868
  0.0 5.6 %copy-start.1 = (f32[16,16,128]{2,1,0:T(8,128)S(1)}, f32[16,16,128]{2,1,0:T(8,128)}, u32[]{:S(2)}) copy-start(f32[16,16,128]{2,1,0:T(8,128)} %param.13) | copy-start | bytes 393220
  5.5 0.7 %copy-start.2 = (f32[16,16]{1,0:T(8,128)S(1)}, f32[16,16]{1,0:T(8,128)}, u32[]{:S(2)}) copy-start(f32[16,16]{1,0:T(8,128)} %param.14) | copy-start | bytes 3076
  9.4 12.0 %copy-start.10 = (s32[16,1]{0,1:T(1,128)S(1)}, s32[16,1]{0,1:T(1,128)}, u32[]{:S(2)}) copy-start(s32[16,1]{0,1:T(1,128)} %param.17) | copy-start | bytes 196
  9.4 12.2 %copy-start.4 = (s32[16,16]{1,0:T(8,128)S(1)}, s32[16,16]{1,0:T(8,128)}, u32[]{:S(2)}) copy-start(s32[16,16]{1,0:T(8,128)} %param.16) | copy-start | bytes 3076
  15.1 18.9 %all-to-all-start = ((f32[8,1,12288]{2,1,0:T(1,128)}), f32[8,1,12288]{2,1,0:T(1,128)S(1)}, u32[]{:S(2)}, u32[]{:S(2)}) async-start(f32[8,1,12288]{2,1,0:T(1,128)} %reshape.75), calls=%async_computation | async-start | bytes 786432 | tf_op jit(solution)/shard_map/all_to_all | solution.py:61
  33.9 17.6 %all-to-all-start.2 = ((bf16[4,1,64]{2,1,0:T(2,128)(2,1)}), bf16[4,1,64]{2,1,0:T(2,128)(2,1)S(1)}, u32[]{:S(2)}, u32[]{:S(2)}) async-start(bf16[4,1,64]{2,1,0:T(2,128)(2,1)} %all_to_all.33), calls=%async_computation.2 | async-start | bytes 4096 | tf_op jit(solution)/shard_map/all_to_all | solution.py:89
  47.3 2.5 %copy-start.3 = (f32[128,128]{1,0:T(8,128)S(1)}, f32[128,128]{1,0:T(8,128)}, u32[]{:S(2)}) copy-start(f32[128,128]{1,0:T(8,128)} %param.15) | copy-start | bytes 196612
  47.3 13.4 %copy-start.5 = (bf16[1,256,512]{2,1,0:T(8,128)(2,1)S(1)}, bf16[1,256,512]{2,1,0:T(8,128)(2,1)}, u32[]{:S(2)}) copy-start(bf16[1,256,512]{2,1,0:T(8,128)(2,1)} %param.18) | copy-start | bytes 786436
  47.3 13.4 %copy-start.9 = (f32[1,512]{1,0:T(1,128)S(1)}, f32[1,512]{1,0:T(1,128)}, u32[]{:S(2)}) copy-start(f32[1,512]{1,0:T(1,128)} %param.19) | copy-start | bytes 6148
  49.8 11.2 %copy-start.6 = (bf16[1,512,256]{2,1,0:T(8,128)(2,1)S(1)}, bf16[1,512,256]{2,1,0:T(8,128)(2,1)}, u32[]{:S(2)}) copy-start(bf16[1,512,256]{2,1,0:T(8,128)(2,1)} %param.21) | copy-start | bytes 786436
  51.5 9.2 %all-to-all-start.1 = ((bf16[4,64,256]{2,1,0:T(8,128)(2,1)}), bf16[4,64,256]{2,1,0:T(8,128)(2,1)S(1)}, u32[]{:S(2)}, u32[]{:S(2)}) async-start(bf16[4,64,256]{2,1,0:T(8,128)(2,1)} %reshape.54), calls=%async_computation.1 | async-start | bytes 262144 | tf_op jit(solution)/shard_map/all_to_all | solution.py:88
  55.7 5.9 %copy-start.7 = (bf16[1,512,256]{2,1,0:T(8,128)(2,1)S(1)}, bf16[1,512,256]{2,1,0:T(8,128)(2,1)}, u32[]{:S(2)}) copy-start(bf16[1,512,256]{2,1,0:T(8,128)(2,1)} %param.23) | copy-start | bytes 786436
  55.7 5.9 %copy-start.8 = (bf16[1,256,512]{2,1,0:T(8,128)(2,1)S(1)}, bf16[1,256,512]{2,1,0:T(8,128)(2,1)}, u32[]{:S(2)}) copy-start(bf16[1,256,512]{2,1,0:T(8,128)(2,1)} %param.22) | copy-start | bytes 786436
where the time goes:
time: 71.2 us; the launch traced here: 70.7 us
  local copies, waits for them, and re-layouts  19.9 us (28%)
  waiting for transfers between devices  16.4 us (23%)
  starting transfers between devices  14.3 us (20%)
  other arithmetic  10.1 us (14%)
  blocking collectives  7.41 us (10%)
  matrix products  2.21 us (3%)
    all_to_all x1, waiting for transfers between devices, shards(): lax.all_to_all(fields, 'lev', split_axis=3, concat_axis=1, tiled=True)  11.5 us
    all_to_all x3, local copies, waits for them, and re-layouts, shards(): lax.all_to_all(fields, 'lev', split_axis=3, concat_axis=1, tiled=True)  7.82 us
    all_to_all x1, blocking collectives, shards(): lax.all_to_all(owner_sum.reshape(groups, most_blocks * BLK, 2 * LEV), 'la...  7.41 us
    all_to_all x1, starting transfers between devices, shards(): lax.all_to_all(fields, 'lev', split_axis=3, concat_axis=1, tiled=True)  6.35 us
    unnamed x25, local copies, waits for them, and re-layouts  6.22 us
    all_to_all x1, waiting for transfers between devices, shards(): lax.all_to_all(outgoing, 'lat', split_axis=0, concat_axis=0, tiled=True)  4.91 us
    all_to_all x1, starting transfers between devices, shards(): lax.all_to_all(outgoing, 'lat', split_axis=0, concat_axis=0, tiled=True)  4.19 us
    all_to_all x1, starting transfers between devices, shards(): lax.all_to_all(sent_factor, 'lat', split_axis=0, concat_axis=0, tiled=True)  3.72 us
  transfers between devices with their start and end apart: 3, of which 2 were waited for; matrix products, arithmetic and copies ran while one was open for 17% of the time, Pallas kernels for 0%

commit v1 on v0

--- a/solution.py
+++ b/solution.py
@@ -1,6 +1,10 @@
+import functools
+
 import jax
 import jax.numpy as jnp
 from jax import lax
+from jax.experimental import pallas as pl
+from jax.experimental.pallas import tpu as pltpu
 from jax.sharding import PartitionSpec as P
 
 LEV = 128
@@ -42,7 +46,7 @@
     return (main_out, side_out)
 
 
-def shards(
+def shards_plain(
     tracers,
     layer_mass,
     courant,
@@ -117,6 +121,331 @@
     return mixing + update
 
 
+MESH = pl.DeviceIdType.MESH
+LANES = 128
+SUBLANES = 8
+PACK = 16
+
+
+def as_columns(rows):
+    count, width = rows.shape
+    shape = (width, width)
+    on_diagonal = lax.broadcasted_iota(jnp.int32, shape, 0) == lax.broadcasted_iota(
+        jnp.int32, shape, 1
+    )
+    return [
+        jnp.sum(
+            jnp.where(on_diagonal, jnp.broadcast_to(rows[i : i + 1, :], shape), 0.0),
+            axis=1,
+            keepdims=True,
+        )
+        for i in range(count)
+    ]
+
+
+def transport(fields, speeds):
+    weight = 0.5 * speeds * (1.0 - speeds)
+    for substep in range(SUBSTEPS):
+        ahead = pltpu.roll(fields, LANES - 1, 1) - fields
+        behind = pltpu.roll(ahead, 1, 1)
+        slopes = jnp.maximum(jnp.minimum(ahead, behind), 0.0) + jnp.minimum(
+            jnp.maximum(ahead, behind), 0.0
+        )
+        fluxes = speeds * fields + weight * slopes
+        fields = fields - (fluxes - pltpu.roll(fluxes, 1, 1))
+    return fields
+
+
+def swap_groups(block, width):
+    rows = block.shape[0]
+    group = lax.broadcasted_iota(jnp.int32, (1, 1, LANES), 2) // width
+    block = pltpu.roll(block, 0, 1, stride=width, stride_axis=0)
+    block = block.reshape(rows // SUBLANES, SUBLANES, LANES)
+    for bit in (1, 2, 4):
+        moved = pltpu.roll(block, SUBLANES - bit, 1)
+        block = jnp.where((group // bit) % 2 == 1, moved, block)
+    block = block.reshape(rows, LANES)
+    return pltpu.roll(block, 0, 1, stride=width, stride_axis=0)
+
+
+def silu(v):
+    half = 0.5 * v
+    return half + half * jnp.tanh(half)
+
+
+def step_kernel(
+    groups,
+    peers,
+    most,
+    tracers,
+    layer_mass,
+    courant,
+    remap,
+    cost_class,
+    spans,
+    b_up,
+    w_up,
+    w_mid,
+    w_down,
+    sw_up,
+    sw_down,
+    out,
+    v_up,
+    v_mid,
+    v_down,
+    v_sup,
+    v_sdown,
+    turned,
+    packed,
+    gathered,
+    factor_out,
+    factor_in,
+    columns_out,
+    columns_in,
+    result_out,
+    result_in,
+    weight_sems,
+    own_sems,
+    lev_send,
+    lev_recv,
+    lat_send,
+    lat_recv,
+):
+    levels, lats, _ = layer_mass.shape
+    me, home = lax.axis_index("lev"), lax.axis_index("lat")
+    width = LANES // peers
+    n_columns = lats * width
+    n_blocks = n_columns // BLK
+    rows = most * BLK
+
+    barrier = pltpu.get_barrier_semaphore()
+    for o in range(1, peers):
+        pl.semaphore_signal(
+            barrier, inc=1, device_id={"lev": lax.rem(me + o, peers)}, device_id_type=MESH
+        )
+    for o in range(1, groups):
+        pl.semaphore_signal(
+            barrier, inc=1, device_id={"lat": lax.rem(home + o, groups)}, device_id_type=MESH
+        )
+    weights = [
+        pltpu.make_async_copy(source, held, weight_sems.at[i])
+        for i, (source, held) in enumerate(
+            ((w_up, v_up), (sw_up, v_sup), (w_mid, v_mid), (w_down, v_down), (sw_down, v_sdown))
+        )
+    ]
+    for copy in weights:
+        copy.start()
+
+    def exchange(stage, source, landing):
+        copies = []
+        for o in range(1, groups):
+            to = lax.rem(home + o, groups)
+            copies.append(
+                pltpu.make_async_remote_copy(
+                    src_ref=source.at[to],
+                    dst_ref=landing.at[home],
+                    send_sem=lat_send.at[stage, o - 1],
+                    recv_sem=lat_recv.at[stage, o - 1],
+                    device_id={"lat": to},
+                    device_id_type=MESH,
+                )
+            )
+        own = pltpu.make_async_copy(source.at[home], landing.at[home], own_sems.at[stage])
+        for copy in copies:
+            copy.start()
+        own.start()
+        return own, copies
+
+    named = [spans[b, 0] for b in range(n_blocks)]
+    slot = []
+    for b in range(n_blocks):
+        rank = jnp.int32(0)
+        for earlier in range(b):
+            rank = rank + (named[earlier] == named[b]).astype(jnp.int32)
+        slot.append((named[b] * most + rank) * BLK)
+    lane = lax.broadcasted_iota(jnp.int32, (1, n_columns), 1)
+    row_of = jnp.zeros((1, n_columns), jnp.int32)
+    for b in range(n_blocks):
+        row_of = jnp.where(lane // BLK == b, slot[b], row_of)
+    row_of = row_of + lane % BLK
+    spread = (groups * rows, n_columns)
+    placing = jnp.where(lax.broadcasted_iota(jnp.int32, spread, 0) == row_of, 1.0, 0.0).astype(
+        jnp.bfloat16
+    )
+    day = jnp.concatenate(
+        [
+            jnp.broadcast_to(column, (width, LANES))
+            for column in as_columns(cost_class[...].astype(jnp.float32) * 0.5)
+        ],
+        axis=0,
+    ).astype(jnp.bfloat16)
+    factor_out[...] = (
+        jnp.dot(placing, day, preferred_element_type=jnp.float32)
+        .astype(jnp.bfloat16)
+        .reshape(factor_out.shape)
+    )
+
+    speeds = as_columns(courant[...])
+    chunk = 4
+    for first in range(0, levels, chunk):
+        speed = jnp.concatenate(
+            [jnp.broadcast_to(speeds[first + i], (lats, LANES)) for i in range(chunk)], axis=0
+        )
+        mass = layer_mass[first : first + chunk].reshape(chunk * lats, LANES)
+        for f in range(3):
+            field = mass
+            if f:
+                field = tracers[f - 1, first : first + chunk].reshape(chunk * lats, LANES) * mass
+            field = swap_groups(transport(field, speed), width)
+            field = field.reshape(chunk, lats // SUBLANES, SUBLANES, LANES)
+            for half in range(lats // SUBLANES):
+                turned[f, half, first * SUBLANES : (first + chunk) * SUBLANES, :] = field[
+                    :, half
+                ].reshape(chunk * SUBLANES, LANES)
+    for d in range(peers):
+        for f in range(3):
+            for half in range(lats // SUBLANES):
+                packed[
+                    d, f * levels : (f + 1) * levels, half * LANES : (half + 1) * LANES
+                ] = turned[f, half, pl.ds(d, levels, stride=SUBLANES), :].astype(jnp.bfloat16)
+
+    pl.semaphore_wait(barrier, peers - 1 + groups - 1)
+    over_lev = []
+    for o in range(1, peers):
+        to = lax.rem(me + o, peers)
+        over_lev.append(
+            pltpu.make_async_remote_copy(
+                src_ref=packed.at[lax.rem(peers - to, peers)],
+                dst_ref=gathered.at[me],
+                send_sem=lev_send.at[o - 1],
+                recv_sem=lev_recv.at[o - 1],
+                device_id={"lev": to},
+                device_id_type=MESH,
+            )
+        )
+        over_lev[-1].start()
+    own_lev = pltpu.make_async_copy(
+        packed.at[lax.rem(peers - me, peers)], gathered.at[me], own_sems.at[3]
+    )
+    own_lev.start()
+    own_factor, over_factor = exchange(0, factor_out, factor_in)
+    own_lev.wait()
+    for copy in over_lev:
+        copy.wait_recv()
+
+    weight = remap[...].astype(jnp.bfloat16)
+    target = [
+        jnp.dot(
+            weight,
+            gathered[:, f * levels : (f + 1) * levels, :].reshape(peers * levels, n_columns),
+            preferred_element_type=jnp.float32,
+        )
+        for f in range(3)
+    ]
+    inverse = 1.0 / target[0]
+    mixing = jnp.concatenate([target[1] * inverse, target[2] * inverse], axis=0)
+    columns_out[...] = (
+        lax.dot_general(
+            placing,
+            mixing.astype(jnp.bfloat16),
+            (((1,), (1,)), ((), ())),
+            preferred_element_type=jnp.float32,
+        )
+        .astype(jnp.bfloat16)
+        .reshape(columns_out.shape)
+    )
+    own_columns, over_columns = exchange(1, columns_out, columns_in)
+    out[...] = mixing
+    own_factor.wait()
+    for copy in over_factor:
+        copy.wait_recv()
+    for copy in weights:
+        copy.wait()
+    own_columns.wait()
+    for copy in over_columns:
+        copy.wait_recv()
+
+    def dot(a, b):
+        return jnp.dot(a, b[0], preferred_element_type=jnp.float32)
+
+    features = columns_in[...].reshape(groups * rows, mixing.shape[0])
+    hidden = silu(dot(features, v_up) + b_up[...]).astype(jnp.bfloat16)
+    shortwave = silu(dot(features, v_sup)).astype(jnp.bfloat16)
+    deeper = silu(dot(hidden, v_mid)).astype(jnp.bfloat16)
+    scale = factor_in[...].reshape(groups * rows, LANES).astype(jnp.float32)
+    scale = jnp.concatenate([scale] * (mixing.shape[0] // LANES), axis=1)
+    result = dot(deeper, v_down) + scale * dot(shortwave, v_sdown)
+    result_out[...] = result.astype(jnp.bfloat16).reshape(result_out.shape)
+    own_result, over_result = exchange(2, result_out, result_in)
+    own_result.wait()
+    for copy in over_result:
+        copy.wait_recv()
+    update = lax.dot_general(
+        result_in[...].reshape(groups * rows, mixing.shape[0]),
+        placing,
+        (((0,), (0,)), ((), ())),
+        preferred_element_type=jnp.float32,
+    )
+    out[...] = out[...] + update
+    for copy in over_lev + over_factor + over_columns + over_result:
+        copy.wait_send()
+
+
+def shards_kernel(groups, peers, tracers, layer_mass, courant, remap, cost_class, spans, w_up, b_up, w_mid, w_down, sw_up, sw_down):
+    levels, lats, lons = layer_mass.shape
+    width = lons // peers
+    n_columns = lats * width
+    n_blocks = n_columns // BLK
+    most = max(2, (n_blocks + groups - 1) // groups)
+    rows = most * BLK
+    n_features = 2 * levels * peers
+    bf16 = jnp.bfloat16
+    vmem = pl.BlockSpec(memory_space=pltpu.VMEM)
+    hbm = pl.BlockSpec(memory_space=pl.ANY)
+    out = pl.pallas_call(
+        functools.partial(step_kernel, groups, peers, most),
+        out_shape=jax.ShapeDtypeStruct((n_features, n_columns), jnp.float32),
+        in_specs=[vmem] * 5 + [pl.BlockSpec(memory_space=pltpu.SMEM), vmem] + [hbm] * 5,
+        out_specs=vmem,
+        scratch_shapes=[
+            pltpu.VMEM(w_up.shape, bf16),
+            pltpu.VMEM(w_mid.shape, bf16),
+            pltpu.VMEM(w_down.shape, bf16),
+            pltpu.VMEM(sw_up.shape, bf16),
+            pltpu.VMEM(sw_down.shape, bf16),
+            pltpu.VMEM((3, lats // SUBLANES, levels * SUBLANES, LANES), jnp.float32),
+            pltpu.VMEM((peers, 3 * levels, n_columns), bf16),
+            pltpu.VMEM((peers, 3 * levels, n_columns), bf16),
+            pltpu.VMEM((groups, rows, LANES), bf16),
+            pltpu.VMEM((groups, rows, LANES), bf16),
+            pltpu.VMEM((groups, rows, n_features), bf16),
+            pltpu.VMEM((groups, rows, n_features), bf16),
+            pltpu.VMEM((groups, rows, n_features), bf16),
+            pltpu.VMEM((groups, rows, n_features), bf16),
+            pltpu.SemaphoreType.DMA((5,)),
+            pltpu.SemaphoreType.DMA((4,)),
+            pltpu.SemaphoreType.DMA((peers - 1,)),
+            pltpu.SemaphoreType.DMA((peers - 1,)),
+            pltpu.SemaphoreType.DMA((3, groups - 1)),
+            pltpu.SemaphoreType.DMA((3, groups - 1)),
+        ],
+        compiler_params=pltpu.CompilerParams(collective_id=0, has_side_effects=True),
+    )(tracers, layer_mass, courant, remap, cost_class, spans, b_up, w_up, w_mid, w_down, sw_up, sw_down)
+    return out.reshape(2, levels * peers, lats, width)
+
+
+def shards(groups, peers, *args):
+    levels, lats, lons = args[1].shape
+    fits = (
+        lons == LANES
+        and peers == SUBLANES
+        and levels % PACK == 0
+        and lats % PACK == 0
+        and lons // peers == BLK
+    )
+    return shards_kernel(groups, peers, *args) if fits else shards_plain(*args)
+
+
 def solution(mesh):
     placed = (
         P(None, "lev", "lat", None),
@@ -133,5 +462,5 @@
         P("lat", None, None),
     )
     return jax.shard_map(
-        shards, mesh=mesh, in_specs=placed, out_specs=P(None, None, "lat", "lev"), check_vma=False
-    )
+        functools.partial(shards, mesh.shape["lat"], mesh.shape["lev"]), mesh=mesh, in_specs=placed, out_specs=P(None, None, "lat", "lev"), check_vma=False
+    )

time: 71.2 us -> 26.8 us (0.38)
  Pallas kernels: 0 us -> 23.4 us
  local copies, waits for them, and re-layouts: 19.9 us -> 3.26 us
  waiting for transfers between devices: 16.4 us -> 0 us
  starting transfers between devices: 14.3 us -> 0 us
  other arithmetic: 10.1 us -> 0 us
  blocking collectives: 7.41 us -> 0 us
  matrix products: 2.21 us -> 0 us
    pallas_call x0 -> x1, Pallas kernels: none -> 23.4 us  [shards_kernel(): pl.pallas_call(functools.partial(step_kernel, groups, peers, most), out_s...]
    all_to_all x3 -> x0, waiting for transfers between devices: 16.4 us -> none  [the longest x1 11.5 us: shards(): lax.all_to_all(fields, 'lev', split_axis=3, concat_axis=1, tiled=True)]
    all_to_all x3 -> x0, starting transfers between devices: 14.3 us -> none  [the longest x1 6.35 us: shards(): lax.all_to_all(fields, 'lev', split_axis=3, concat_axis=1, tiled=True)]
    all_to_all x4 -> x0, local copies, waits for them, and re-layouts: 8.5 us -> none  [the longest x3 7.82 us: shards(): lax.all_to_all(fields, 'lev', split_axis=3, concat_axis=1, tiled=True)]
    all_to_all x1 -> x0, blocking collectives: 7.41 us -> none  [shards(): lax.all_to_all(owner_sum.reshape(groups, most_blocks * BLK, 2 * LEV), 'la...]
    unnamed x25 -> x1, local copies, waits for them, and re-layouts: 6.22 us -> 1.33 us
    mul x6 -> x0, other arithmetic: 4.56 us -> none  [the longest x5 3.49 us: advect(): fluxes = speeds * (fields + 0.5 * (1.0 - speeds) * slopes)]
    concatenate x2 -> x0, other arithmetic: 2.3 us -> none  [shards(): jnp.concatenate([layer_mass[None], tracers * layer_mass[None]], axis=0)]
  transfers between devices with their start and end apart: 3 -> 0, of which waited for: 2 -> 0; matrix products, arithmetic and copies ran while one was open for 17% -> 0% of each run, Pallas kernels for 0% -> 0%
where the time goes in v1:
time: 26.8 us; the launch traced here: 26.7 us
  Pallas kernels  23.4 us (87%)
  local copies, waits for them, and re-layouts  3.26 us (12%)
    pallas_call x1, Pallas kernels, shards_kernel(): pl.pallas_call(functools.partial(step_kernel, groups, peers, most), out_s...  23.4 us
    unnamed x1, local copies, waits for them, and re-layouts  1.33 us
    pallas_call x1, local copies, waits for them, and re-layouts, shards_kernel(): pl.pallas_call(functools.partial(step_kernel, groups, peers, most), out_s...  1.08 us
    reshape x2, local copies, waits for them, and re-layouts, shards_kernel(): return out.reshape(2, levels * peers, lats, width)  0.86 us

profile of v1, /device:TPU:0, one launch (start us, length us, event | category | flops | bytes accessed | tf_op | source)
XLA Modules:
  0.0 26.7 jit_solution(9701436333258307150)
XLA Ops:
  0.0 1.3 %copy.15.spans = s32[16,1]{1,0:T(8,128)} copy(s32[16,1]{0,1:T(1,128)} %param.17) | data formatting | bytes 128 | tf_op args[5]
  1.3 23.4 %shard_map.118 = f32[256,256]{1,0:T(8,128)} custom-call(f32[2,16,16,128]{3,2,1,0:T(8,128)} %tracers.1, f32[16,16,128]{2,1,0:T(8,128)} %layer_mass.1, f32[16,16]{1,0:T(8,128)} %courant.1, f32[128,128]{1,0:T(8,128)} %remap.1, s32[16,16]{1,0:T(8,128)} %cost_class.1, s32[16,1]{1,0:T(8,128)} %copy.15.spans, f32[1,512]{1,0:T(1,128)} %b_up.1, ...), custom_call_target="tpu_custom_call" | custom-call | tf_op jit(solution)/shard_map/pallas_call | solution.py:405
  24.7 1.1 %copy.16 = f32[256,256]{0,1:T(8,128)S(1)} copy(f32[256,256]{1,0:T(8,128)} %shard_map.118) | data formatting | bytes 524288 | tf_op jit(solution)/shard_map/pallas_call | solution.py:405
  25.8 0.1 reshape.3
  26.0 0.7 %copy.17 = f32[2,128,16,16]{1,3,2,0:T(8,128)} copy(f32[2,128,16,16]{1,0,3,2:T(2,128)S(1)} %reshape.3) | data formatting | bytes 524288 | tf_op jit(solution)/shard_map/reshape | solution.py:434

commit v2 on v1

--- a/solution.py
+++ b/solution.py
@@ -147,7 +147,7 @@
     weight = 0.5 * speeds * (1.0 - speeds)
     for substep in range(SUBSTEPS):
         ahead = pltpu.roll(fields, LANES - 1, 1) - fields
-        behind = pltpu.roll(ahead, 1, 1)
+        behind = fields - pltpu.roll(fields, 1, 1)
         slopes = jnp.maximum(jnp.minimum(ahead, behind), 0.0) + jnp.minimum(
             jnp.maximum(ahead, behind), 0.0
         )
@@ -256,7 +256,7 @@
         own.start()
         return own, copies
 
-    named = [spans[b, 0] for b in range(n_blocks)]
+    named = [spans[0, b] for b in range(n_blocks)]
     slot = []
     for b in range(n_blocks):
         rank = jnp.int32(0)
@@ -272,6 +272,12 @@
     placing = jnp.where(lax.broadcasted_iota(jnp.int32, spread, 0) == row_of, 1.0, 0.0).astype(
         jnp.bfloat16
     )
+    offset = lax.broadcasted_iota(jnp.int32, (BLK, groups * rows), 1) - lax.broadcasted_iota(
+        jnp.int32, (BLK, groups * rows), 0
+    )
+    restoring = jnp.concatenate(
+        [jnp.where(offset == slot[b], 1.0, 0.0) for b in range(n_blocks)], axis=0
+    ).astype(jnp.bfloat16)
     day = jnp.concatenate(
         [
             jnp.broadcast_to(column, (width, LANES))
@@ -285,77 +291,82 @@
         .reshape(factor_out.shape)
     )
 
-    speeds = as_columns(courant[...])
-    chunk = 4
-    for first in range(0, levels, chunk):
-        speed = jnp.concatenate(
-            [jnp.broadcast_to(speeds[first + i], (lats, LANES)) for i in range(chunk)], axis=0
-        )
-        mass = layer_mass[first : first + chunk].reshape(chunk * lats, LANES)
-        for f in range(3):
-            field = mass
-            if f:
-                field = tracers[f - 1, first : first + chunk].reshape(chunk * lats, LANES) * mass
-            field = swap_groups(transport(field, speed), width)
-            field = field.reshape(chunk, lats // SUBLANES, SUBLANES, LANES)
+    speed = jnp.concatenate(
+        [jnp.broadcast_to(column, (lats, LANES)) for column in as_columns(courant[...])], axis=0
+    )
+    mass = layer_mass[...].reshape(levels * lats, LANES)
+    side = me // (peers // 2)
+    others = []
+    for k in range(peers - 1):
+        low = peers - 1 - k
+        low = low - (low <= me).astype(jnp.int32)
+        high = k + (k >= me).astype(jnp.int32)
+        others.append(side * high + (1 - side) * low)
+    over_lev = []
+    for f in range(3):
+        field = mass
+        if f:
+            field = tracers[f - 1].reshape(levels * lats, LANES) * mass
+        field = swap_groups(transport(field, speed), width)
+        field = field.reshape(levels, lats // SUBLANES, SUBLANES, LANES)
+        for half in range(lats // SUBLANES):
+            turned[f, half] = field[:, half].reshape(levels * SUBLANES, LANES)
+        for d in range(peers):
             for half in range(lats // SUBLANES):
-                turned[f, half, first * SUBLANES : (first + chunk) * SUBLANES, :] = field[
-                    :, half
-                ].reshape(chunk * SUBLANES, LANES)
-    for d in range(peers):
-        for f in range(3):
-            for half in range(lats // SUBLANES):
-                packed[
-                    d, f * levels : (f + 1) * levels, half * LANES : (half + 1) * LANES
-                ] = turned[f, half, pl.ds(d, levels, stride=SUBLANES), :].astype(jnp.bfloat16)
-
-    pl.semaphore_wait(barrier, peers - 1 + groups - 1)
-    over_lev = []
-    for o in range(1, peers):
-        to = lax.rem(me + o, peers)
-        over_lev.append(
-            pltpu.make_async_remote_copy(
-                src_ref=packed.at[lax.rem(peers - to, peers)],
-                dst_ref=gathered.at[me],
-                send_sem=lev_send.at[o - 1],
-                recv_sem=lev_recv.at[o - 1],
+                packed[f, d, :, half * LANES : (half + 1) * LANES] = turned[
+                    f, half, pl.ds(d, levels, stride=SUBLANES), :
+                ].astype(jnp.bfloat16)
+        if f == 0:
+            pl.semaphore_wait(barrier, peers - 1 + groups - 1)
+        copies = []
+        for k, to in enumerate(others):
+            copy = pltpu.make_async_remote_copy(
+                src_ref=packed.at[f, lax.rem(peers - to, peers)],
+                dst_ref=gathered.at[f, me],
+                send_sem=lev_send.at[f, k],
+                recv_sem=lev_recv.at[f, me],
                 device_id={"lev": to},
                 device_id_type=MESH,
             )
-        )
-        over_lev[-1].start()
-    own_lev = pltpu.make_async_copy(
-        packed.at[lax.rem(peers - me, peers)], gathered.at[me], own_sems.at[3]
-    )
-    own_lev.start()
+            copy.start()
+            copies.append(copy)
+        own = pltpu.make_async_copy(
+            packed.at[f, lax.rem(peers - me, peers)], gathered.at[f, me], own_sems.at[3 + f]
+        )
+        own.start()
+        over_lev.append((own, copies))
     own_factor, over_factor = exchange(0, factor_out, factor_in)
-    own_lev.wait()
-    for copy in over_lev:
-        copy.wait_recv()
-
     weight = remap[...].astype(jnp.bfloat16)
-    target = [
-        jnp.dot(
-            weight,
-            gathered[:, f * levels : (f + 1) * levels, :].reshape(peers * levels, n_columns),
-            preferred_element_type=jnp.float32,
-        )
-        for f in range(3)
-    ]
+    target = []
+    for f in range(3):
+        over_lev[f][0].wait()
+        for k, source in enumerate(others):
+            pltpu.make_async_remote_copy(
+                src_ref=packed.at[f, 0],
+                dst_ref=gathered.at[f, source],
+                send_sem=lev_send.at[f, k],
+                recv_sem=lev_recv.at[f, source],
+                device_id={"lev": source},
+                device_id_type=MESH,
+            ).wait_recv()
+        target.append(
+            lax.dot_general(
+                gathered[f].reshape(peers * levels, n_columns),
+                weight,
+                (((0,), (1,)), ((), ())),
+                preferred_element_type=jnp.float32,
+            )
+        )
     inverse = 1.0 / target[0]
-    mixing = jnp.concatenate([target[1] * inverse, target[2] * inverse], axis=0)
+    mixing = jnp.concatenate([target[1] * inverse, target[2] * inverse], axis=1)
     columns_out[...] = (
-        lax.dot_general(
-            placing,
-            mixing.astype(jnp.bfloat16),
-            (((1,), (1,)), ((), ())),
-            preferred_element_type=jnp.float32,
-        )
+        jnp.dot(placing, mixing.astype(jnp.bfloat16), preferred_element_type=jnp.float32)
         .astype(jnp.bfloat16)
         .reshape(columns_out.shape)
     )
     own_columns, over_columns = exchange(1, columns_out, columns_in)
-    out[...] = mixing
+    for t in range(2):
+        out[t] = mixing[:, t * LANES : (t + 1) * LANES]
     own_factor.wait()
     for copy in over_factor:
         copy.wait_recv()
@@ -368,27 +379,30 @@
     def dot(a, b):
         return jnp.dot(a, b[0], preferred_element_type=jnp.float32)
 
-    features = columns_in[...].reshape(groups * rows, mixing.shape[0])
+    features = columns_in[...].reshape(groups * rows, mixing.shape[1])
     hidden = silu(dot(features, v_up) + b_up[...]).astype(jnp.bfloat16)
     shortwave = silu(dot(features, v_sup)).astype(jnp.bfloat16)
     deeper = silu(dot(hidden, v_mid)).astype(jnp.bfloat16)
     scale = factor_in[...].reshape(groups * rows, LANES).astype(jnp.float32)
-    scale = jnp.concatenate([scale] * (mixing.shape[0] // LANES), axis=1)
+    scale = jnp.concatenate([scale] * (mixing.shape[1] // LANES), axis=1)
     result = dot(deeper, v_down) + scale * dot(shortwave, v_sdown)
     result_out[...] = result.astype(jnp.bfloat16).reshape(result_out.shape)
     own_result, over_result = exchange(2, result_out, result_in)
     own_result.wait()
     for copy in over_result:
         copy.wait_recv()
-    update = lax.dot_general(
-        result_in[...].reshape(groups * rows, mixing.shape[0]),
-        placing,
-        (((0,), (0,)), ((), ())),
+    update = jnp.dot(
+        restoring,
+        result_in[...].reshape(groups * rows, mixing.shape[1]),
         preferred_element_type=jnp.float32,
     )
-    out[...] = out[...] + update
-    for copy in over_lev + over_factor + over_columns + over_result:
+    for t in range(2):
+        out[t] = out[t] + update[:, t * LANES : (t + 1) * LANES]
+    for copy in over_factor + over_columns + over_result:
         copy.wait_send()
+    for own, copies in over_lev:
+        for copy in copies:
+            copy.wait_send()
 
 
 def shards_kernel(groups, peers, tracers, layer_mass, courant, remap, cost_class, spans, w_up, b_up, w_mid, w_down, sw_up, sw_down):
@@ -404,7 +418,7 @@
     hbm = pl.BlockSpec(memory_space=pl.ANY)
     out = pl.pallas_call(
         functools.partial(step_kernel, groups, peers, most),
-        out_shape=jax.ShapeDtypeStruct((n_features, n_columns), jnp.float32),
+        out_shape=jax.ShapeDtypeStruct((2, n_columns, levels * peers), jnp.float32),
         in_specs=[vmem] * 5 + [pl.BlockSpec(memory_space=pltpu.SMEM), vmem] + [hbm] * 5,
         out_specs=vmem,
         scratch_shapes=[
@@ -414,8 +428,8 @@
             pltpu.VMEM(sw_up.shape, bf16),
             pltpu.VMEM(sw_down.shape, bf16),
             pltpu.VMEM((3, lats // SUBLANES, levels * SUBLANES, LANES), jnp.float32),
-            pltpu.VMEM((peers, 3 * levels, n_columns), bf16),
-            pltpu.VMEM((peers, 3 * levels, n_columns), bf16),
+            pltpu.VMEM((3, peers, levels, n_columns), bf16),
+            pltpu.VMEM((3, peers, levels, n_columns), bf16),
             pltpu.VMEM((groups, rows, LANES), bf16),
             pltpu.VMEM((groups, rows, LANES), bf16),
             pltpu.VMEM((groups, rows, n_features), bf16),
@@ -423,15 +437,15 @@
             pltpu.VMEM((groups, rows, n_features), bf16),
             pltpu.VMEM((groups, rows, n_features), bf16),
             pltpu.SemaphoreType.DMA((5,)),
-            pltpu.SemaphoreType.DMA((4,)),
-            pltpu.SemaphoreType.DMA((peers - 1,)),
-            pltpu.SemaphoreType.DMA((peers - 1,)),
+            pltpu.SemaphoreType.DMA((6,)),
+            pltpu.SemaphoreType.DMA((3, peers - 1)),
+            pltpu.SemaphoreType.DMA((3, peers)),
             pltpu.SemaphoreType.DMA((3, groups - 1)),
             pltpu.SemaphoreType.DMA((3, groups - 1)),
         ],
         compiler_params=pltpu.CompilerParams(collective_id=0, has_side_effects=True),
-    )(tracers, layer_mass, courant, remap, cost_class, spans, b_up, w_up, w_mid, w_down, sw_up, sw_down)
-    return out.reshape(2, levels * peers, lats, width)
+    )(tracers, layer_mass, courant, remap, cost_class, spans.reshape(1, -1), b_up, w_up, w_mid, w_down, sw_up, sw_down)
+    return out.reshape(2, lats, width, levels * peers).transpose(0, 3, 1, 2)
 
 
 def shards(groups, peers, *args):
@@ -442,6 +456,7 @@
         and levels % PACK == 0
         and lats % PACK == 0
         and lons // peers == BLK
+        and levels * peers == LANES
     )
     return shards_kernel(groups, peers, *args) if fits else shards_plain(*args)
 

time: 26.8 us -> 24.4 us (0.910)
  local copies, waits for them, and re-layouts: 3.26 us -> 1.67 us
  Pallas kernels: 23.4 us -> 22.5 us
    pallas_call x1 -> x0, local copies, waits for them, and re-layouts: 1.08 us -> none  [shards_kernel(): pl.pallas_call(functools.partial(step_kernel, groups, peers, most), out_s...]
    pallas_call x1, Pallas kernels: 23.4 us -> 22.5 us  [shards_kernel(): pl.pallas_call(functools.partial(step_kernel, groups, peers, most), out_s...]
    reshape x2 -> x0, local copies, waits for them, and re-layouts: 0.86 us -> none  [shards_kernel(): return out.reshape(2, levels * peers, lats, width)]
    unnamed x1, local copies, waits for them, and re-layouts: 1.33 us -> 1.67 us
where the time goes in v2:
time: 24.4 us; the launch traced here: 24.2 us
  Pallas kernels  22.5 us (92%)
  local copies, waits for them, and re-layouts  1.67 us (7%)
    pallas_call x1, Pallas kernels, shards_kernel(): pl.pallas_call(functools.partial(step_kernel, groups, peers, most), out_s...  22.5 us
    unnamed x1, local copies, waits for them, and re-layouts  1.67 us

profile of v2, /device:TPU:0, one launch (start us, length us, event | category | flops | bytes accessed | tf_op | source)
XLA Modules:
  0.0 24.2 jit_solution(9149977603467246833)
XLA Ops:
  0.0 22.5 %shard_map.118 = f32[2,256,128]{2,1,0:T(8,128)} custom-call(f32[2,16,16,128]{3,2,1,0:T(8,128)} %tracers.1, f32[16,16,128]{2,1,0:T(8,128)} %layer_mass.1, f32[16,16]{1,0:T(8,128)} %courant.1, f32[128,128]{1,0:T(8,128)} %remap.1, s32[16,16]{1,0:T(8,128)} %cost_class.1, s32[1,16]{1,0:T(1,128)} %bitcast.5, f32[1,512]{1,0:T(1,128)} %b_up.1, ...), custom_call_target="tpu_custom_call" | custom-call | tf_op jit(solution)/shard_map/pallas_call | solution.py:419
  22.5 1.7 %copy.14 = f32[2,128,16,16]{1,3,2,0:T(8,128)} copy(f32[2,128,16,16]{1,3,2,0:T(8,128)} %bitcast.4) | data formatting | bytes 524288

commit v3 on v2

--- a/solution.py
+++ b/solution.py
@@ -189,7 +189,8 @@
     w_down,
     sw_up,
     sw_down,
-    out,
+    mixing_out,
+    update_out,
     v_up,
     v_mid,
     v_down,
@@ -204,6 +205,7 @@
     columns_in,
     result_out,
     result_in,
+    mixed,
     weight_sems,
     own_sems,
     lev_send,
@@ -236,26 +238,48 @@
     for copy in weights:
         copy.start()
 
-    def exchange(stage, source, landing):
-        copies = []
-        for o in range(1, groups):
-            to = lax.rem(home + o, groups)
-            copies.append(
-                pltpu.make_async_remote_copy(
-                    src_ref=source.at[to],
-                    dst_ref=landing.at[home],
-                    send_sem=lat_send.at[stage, o - 1],
-                    recv_sem=lat_recv.at[stage, o - 1],
-                    device_id={"lat": to},
-                    device_id_type=MESH,
-                )
+    speed = jnp.concatenate(
+        [jnp.broadcast_to(column, (lats, LANES)) for column in as_columns(courant[...])], axis=0
+    )
+    mass = layer_mass[...].reshape(levels * lats, LANES)
+    side = me // (peers // 2)
+    others = []
+    for k in range(peers - 1):
+        low = peers - 1 - k
+        low = low - (low <= me).astype(jnp.int32)
+        high = k + (k >= me).astype(jnp.int32)
+        others.append(side * high + (1 - side) * low)
+    own_lev = []
+    for f in range(3):
+        field = mass
+        if f:
+            field = tracers[f - 1].reshape(levels * lats, LANES) * mass
+        field = swap_groups(transport(field, speed), width)
+        field = field.reshape(levels, lats // SUBLANES, SUBLANES, LANES)
+        for half in range(lats // SUBLANES):
+            turned[f, half] = field[:, half].reshape(levels * SUBLANES, LANES)
+        for d in range(peers):
+            for half in range(lats // SUBLANES):
+                packed[f, d, :, half * LANES : (half + 1) * LANES] = turned[
+                    f, half, pl.ds(d, levels, stride=SUBLANES), :
+                ].astype(jnp.bfloat16)
+        if f == 0:
+            pl.semaphore_wait(barrier, peers - 1 + groups - 1)
+        for to in others:
+            copy = pltpu.make_async_remote_copy(
+                src_ref=packed.at[f, lax.rem(peers - to, peers)],
+                dst_ref=gathered.at[f, me],
+                send_sem=lev_send,
+                recv_sem=lev_recv.at[f],
+                device_id={"lev": to},
+                device_id_type=MESH,
             )
-        own = pltpu.make_async_copy(source.at[home], landing.at[home], own_sems.at[stage])
-        for copy in copies:
             copy.start()
+        own = pltpu.make_async_copy(
+            packed.at[f, lax.rem(peers - me, peers)], gathered.at[f, me], own_sems.at[f]
+        )
         own.start()
-        return own, copies
-
+        own_lev.append(own)
     named = [spans[0, b] for b in range(n_blocks)]
     slot = []
     for b in range(n_blocks):
@@ -291,64 +315,44 @@
         .reshape(factor_out.shape)
     )
 
-    speed = jnp.concatenate(
-        [jnp.broadcast_to(column, (lats, LANES)) for column in as_columns(courant[...])], axis=0
-    )
-    mass = layer_mass[...].reshape(levels * lats, LANES)
-    side = me // (peers // 2)
-    others = []
-    for k in range(peers - 1):
-        low = peers - 1 - k
-        low = low - (low <= me).astype(jnp.int32)
-        high = k + (k >= me).astype(jnp.int32)
-        others.append(side * high + (1 - side) * low)
-    over_lev = []
-    for f in range(3):
-        field = mass
-        if f:
-            field = tracers[f - 1].reshape(levels * lats, LANES) * mass
-        field = swap_groups(transport(field, speed), width)
-        field = field.reshape(levels, lats // SUBLANES, SUBLANES, LANES)
-        for half in range(lats // SUBLANES):
-            turned[f, half] = field[:, half].reshape(levels * SUBLANES, LANES)
-        for d in range(peers):
-            for half in range(lats // SUBLANES):
-                packed[f, d, :, half * LANES : (half + 1) * LANES] = turned[
-                    f, half, pl.ds(d, levels, stride=SUBLANES), :
-                ].astype(jnp.bfloat16)
-        if f == 0:
-            pl.semaphore_wait(barrier, peers - 1 + groups - 1)
-        copies = []
-        for k, to in enumerate(others):
-            copy = pltpu.make_async_remote_copy(
-                src_ref=packed.at[f, lax.rem(peers - to, peers)],
-                dst_ref=gathered.at[f, me],
-                send_sem=lev_send.at[f, k],
-                recv_sem=lev_recv.at[f, me],
-                device_id={"lev": to},
-                device_id_type=MESH,
-            )
-            copy.start()
-            copies.append(copy)
-        own = pltpu.make_async_copy(
-            packed.at[f, lax.rem(peers - me, peers)], gathered.at[f, me], own_sems.at[3 + f]
-        )
-        own.start()
-        over_lev.append((own, copies))
-    own_factor, over_factor = exchange(0, factor_out, factor_in)
+    turn = 1 - 2 * lax.rem(home, 2)
+    partners = [lax.rem(home + turn * o + groups * groups, groups) for o in range(groups - 1, 0, -1)]
+
+    def send(stage, source, landing, arrival, to):
+        copy = pltpu.make_async_remote_copy(
+            src_ref=source.at[to],
+            dst_ref=landing.at[home],
+            send_sem=lat_send.at[stage],
+            recv_sem=arrival,
+            device_id={"lat": to},
+            device_id_type=MESH,
+        )
+        copy.start()
+
+    def all_partners(stage, source, landing, arrival):
+        return pltpu.make_async_remote_copy(
+            src_ref=source.at[pl.ds(0, groups - 1)],
+            dst_ref=landing.at[pl.ds(0, groups - 1)],
+            send_sem=lat_send.at[stage],
+            recv_sem=arrival,
+            device_id={"lat": partners[0]},
+            device_id_type=MESH,
+        )
+
+    for to in partners:
+        send(0, factor_out, factor_in, lat_recv.at[groups], to)
     weight = remap[...].astype(jnp.bfloat16)
     target = []
     for f in range(3):
-        over_lev[f][0].wait()
-        for k, source in enumerate(others):
-            pltpu.make_async_remote_copy(
-                src_ref=packed.at[f, 0],
-                dst_ref=gathered.at[f, source],
-                send_sem=lev_send.at[f, k],
-                recv_sem=lev_recv.at[f, source],
-                device_id={"lev": source},
-                device_id_type=MESH,
-            ).wait_recv()
+        own_lev[f].wait()
+        pltpu.make_async_remote_copy(
+            src_ref=packed.at[f, pl.ds(0, peers - 1)],
+            dst_ref=gathered.at[f, pl.ds(0, peers - 1)],
+            send_sem=lev_send,
+            recv_sem=lev_recv.at[f],
+            device_id={"lev": others[0]},
+            device_id_type=MESH,
+        ).wait_recv()
         target.append(
             lax.dot_general(
                 gathered[f].reshape(peers * levels, n_columns),
@@ -364,45 +368,64 @@
         .astype(jnp.bfloat16)
         .reshape(columns_out.shape)
     )
-    own_columns, over_columns = exchange(1, columns_out, columns_in)
+    for to in partners:
+        send(1, columns_out, columns_in, lat_recv.at[home], to)
     for t in range(2):
-        out[t] = mixing[:, t * LANES : (t + 1) * LANES]
-    own_factor.wait()
-    for copy in over_factor:
-        copy.wait_recv()
+        mixed[t] = mixing[:, t * LANES : (t + 1) * LANES]
+    own_mixed = pltpu.make_async_copy(mixed, mixing_out, own_sems.at[3])
+    own_mixed.start()
     for copy in weights:
         copy.wait()
-    own_columns.wait()
-    for copy in over_columns:
-        copy.wait_recv()
 
     def dot(a, b):
         return jnp.dot(a, b[0], preferred_element_type=jnp.float32)
 
-    features = columns_in[...].reshape(groups * rows, mixing.shape[1])
-    hidden = silu(dot(features, v_up) + b_up[...]).astype(jnp.bfloat16)
-    shortwave = silu(dot(features, v_sup)).astype(jnp.bfloat16)
-    deeper = silu(dot(hidden, v_mid)).astype(jnp.bfloat16)
-    scale = factor_in[...].reshape(groups * rows, LANES).astype(jnp.float32)
-    scale = jnp.concatenate([scale] * (mixing.shape[1] // LANES), axis=1)
-    result = dot(deeper, v_down) + scale * dot(shortwave, v_sdown)
-    result_out[...] = result.astype(jnp.bfloat16).reshape(result_out.shape)
-    own_result, over_result = exchange(2, result_out, result_in)
-    own_result.wait()
-    for copy in over_result:
-        copy.wait_recv()
+    def nets(features, scale):
+        hidden = silu(dot(features, v_up) + b_up[...]).astype(jnp.bfloat16)
+        shortwave = silu(dot(features, v_sup)).astype(jnp.bfloat16)
+        deeper = silu(dot(hidden, v_mid)).astype(jnp.bfloat16)
+        scale = jnp.concatenate([scale.astype(jnp.float32)] * (mixing.shape[1] // LANES), axis=1)
+        return (dot(deeper, v_down) + scale * dot(shortwave, v_sdown)).astype(jnp.bfloat16)
+
+    result_in[home] = nets(columns_out[home], factor_out[home])
+    all_partners(0, factor_out, factor_in, lat_recv.at[groups]).wait_recv()
+    for batch in (partners[:1], partners[1:]):
+        for source in batch:
+            pltpu.make_async_remote_copy(
+                src_ref=columns_out.at[source],
+                dst_ref=columns_in.at[source],
+                send_sem=lat_send.at[1],
+                recv_sem=lat_recv.at[source],
+                device_id={"lat": source},
+                device_id_type=MESH,
+            ).wait_recv()
+        result = nets(
+            jnp.concatenate([columns_in[source] for source in batch], axis=0),
+            jnp.concatenate([factor_in[source] for source in batch], axis=0),
+        )
+        for i, source in enumerate(batch):
+            result_out[source] = result[i * rows : (i + 1) * rows]
+            send(2, result_out, result_in, lat_recv.at[groups + 1], source)
+    all_partners(2, result_out, result_in, lat_recv.at[groups + 1]).wait_recv()
     update = jnp.dot(
         restoring,
         result_in[...].reshape(groups * rows, mixing.shape[1]),
         preferred_element_type=jnp.float32,
     )
     for t in range(2):
-        out[t] = out[t] + update[:, t * LANES : (t + 1) * LANES]
-    for copy in over_factor + over_columns + over_result:
-        copy.wait_send()
-    for own, copies in over_lev:
-        for copy in copies:
-            copy.wait_send()
+        update_out[t] = update[:, t * LANES : (t + 1) * LANES].astype(jnp.bfloat16)
+    own_mixed.wait()
+    all_partners(0, factor_out, factor_in, lat_recv.at[groups]).wait_send()
+    all_partners(1, columns_out, columns_in, lat_recv.at[groups]).wait_send()
+    all_partners(2, result_out, result_in, lat_recv.at[groups]).wait_send()
+    pltpu.make_async_remote_copy(
+        src_ref=packed.at[:, pl.ds(0, peers - 1)],
+        dst_ref=gathered.at[:, pl.ds(0, peers - 1)],
+        send_sem=lev_send,
+        recv_sem=lev_recv.at[0],
+        device_id={"lev": others[0]},
+        device_id_type=MESH,
+    ).wait_send()
 
 
 def shards_kernel(groups, peers, tracers, layer_mass, courant, remap, cost_class, spans, w_up, b_up, w_mid, w_down, sw_up, sw_down):
@@ -416,11 +439,14 @@
     bf16 = jnp.bfloat16
     vmem = pl.BlockSpec(memory_space=pltpu.VMEM)
     hbm = pl.BlockSpec(memory_space=pl.ANY)
-    out = pl.pallas_call(
+    mixing, update = pl.pallas_call(
         functools.partial(step_kernel, groups, peers, most),
-        out_shape=jax.ShapeDtypeStruct((2, n_columns, levels * peers), jnp.float32),
+        out_shape=(
+            jax.ShapeDtypeStruct((2, n_columns, levels * peers), jnp.float32),
+            jax.ShapeDtypeStruct((2, n_columns, levels * peers), bf16),
+        ),
         in_specs=[vmem] * 5 + [pl.BlockSpec(memory_space=pltpu.SMEM), vmem] + [hbm] * 5,
-        out_specs=vmem,
+        out_specs=(hbm, vmem),
         scratch_shapes=[
             pltpu.VMEM(w_up.shape, bf16),
             pltpu.VMEM(w_mid.shape, bf16),
@@ -436,15 +462,17 @@
             pltpu.VMEM((groups, rows, n_features), bf16),
             pltpu.VMEM((groups, rows, n_features), bf16),
             pltpu.VMEM((groups, rows, n_features), bf16),
+            pltpu.VMEM((2, n_columns, levels * peers), jnp.float32),
             pltpu.SemaphoreType.DMA((5,)),
-            pltpu.SemaphoreType.DMA((6,)),
-            pltpu.SemaphoreType.DMA((3, peers - 1)),
-            pltpu.SemaphoreType.DMA((3, peers)),
-            pltpu.SemaphoreType.DMA((3, groups - 1)),
-            pltpu.SemaphoreType.DMA((3, groups - 1)),
+            pltpu.SemaphoreType.DMA((4,)),
+            pltpu.SemaphoreType.DMA,
+            pltpu.SemaphoreType.DMA((3,)),
+            pltpu.SemaphoreType.DMA((3,)),
+            pltpu.SemaphoreType.DMA((groups + 2,)),
         ],
         compiler_params=pltpu.CompilerParams(collective_id=0, has_side_effects=True),
     )(tracers, layer_mass, courant, remap, cost_class, spans.reshape(1, -1), b_up, w_up, w_mid, w_down, sw_up, sw_down)
+    out = mixing + update.astype(jnp.float32)
     return out.reshape(2, lats, width, levels * peers).transpose(0, 3, 1, 2)
 
 

time: 24.4 us -> 23.3 us (0.955)
  other arithmetic: 0 us -> 1.71 us
  local copies, waits for them, and re-layouts: 1.67 us -> 0 us
  Pallas kernels: 22.5 us -> 21.5 us
    add x0 -> x1, other arithmetic: none -> 1.71 us  [shards_kernel(): out = mixing + update.astype(jnp.float32)]
    unnamed x1 -> x0, local copies, waits for them, and re-layouts: 1.67 us -> none
    pallas_call x1, Pallas kernels: 22.5 us -> 21.5 us  [shards_kernel(): pl.pallas_call(functools.partial(step_kernel, groups, peers, most), out_s...]
where the time goes in v3:
time: 23.3 us; the launch traced here: 23.2 us
  Pallas kernels  21.5 us (92%)
  other arithmetic  1.71 us (7%)
    pallas_call x1, Pallas kernels, shards_kernel(): pl.pallas_call(functools.partial(step_kernel, groups, peers, most), out_s...  21.5 us
    add x1, other arithmetic, shards_kernel(): out = mixing + update.astype(jnp.float32)  1.71 us

profile of v3, /device:TPU:0, one launch (start us, length us, event | category | flops | bytes accessed | tf_op | source)
XLA Modules:
  0.0 23.2 jit_solution(15236961790568083338)
XLA Ops:
  0.0 21.5 %shard_map.118 = (f32[2,256,128]{2,1,0:T(8,128)}, bf16[2,256,128]{2,1,0:T(8,128)(2,1)}) custom-call(f32[2,16,16,128]{3,2,1,0:T(8,128)} %tracers.1, f32[16,16,128]{2,1,0:T(8,128)} %layer_mass.1, f32[16,16]{1,0:T(8,128)} %courant.1, f32[128,128]{1,0:T(8,128)} %remap.1, s32[16,16]{1,0:T(8,128)} %cost_class.1, s32[1,16]{1,0:T(1,128)} %bitcast.4, f32[1,512]{1,0:T(1,128)} %b_up.1, ...), custom_call_target="tpu_custom_call" | custom-call | tf_op jit(solution)/shard_map/pallas_call | solution.py:442
  21.5 1.7 %convert_add_fusion = f32[2,256,128]{2,1,0:T(8,128)} fusion(f32[2,256,128]{2,1,0:T(8,128)} %get-tuple-element.7, bf16[2,256,128]{2,1,0:T(8,128)(2,1)} %get-tuple-element.8), kind=kLoop, calls=%fused_computation | loop fusion | flops 131072 | bytes 655360 | tf_op jit(solution)/shard_map/add | solution.py:475

commit v4 on v3

--- a/solution.py
+++ b/solution.py
@@ -470,8 +470,26 @@
             pltpu.SemaphoreType.DMA((3,)),
             pltpu.SemaphoreType.DMA((groups + 2,)),
         ],
-        compiler_params=pltpu.CompilerParams(collective_id=0, has_side_effects=True),
-    )(tracers, layer_mass, courant, remap, cost_class, spans.reshape(1, -1), b_up, w_up, w_mid, w_down, sw_up, sw_down)
+        compiler_params=pltpu.CompilerParams(collective_id=0, has_side_effects=True, vmem_limit_bytes=16 * 1024 * 1024),
+    )(
+        *(
+            pltpu.with_memory_space_constraint(array, pltpu.HBM)
+            for array in (
+                tracers,
+                layer_mass,
+                courant,
+                remap,
+                cost_class,
+                spans.reshape(1, -1),
+                b_up,
+                w_up,
+                w_mid,
+                w_down,
+                sw_up,
+                sw_down,
+            )
+        )
+    )
     out = mixing + update.astype(jnp.float32)
     return out.reshape(2, lats, width, levels * peers).transpose(0, 3, 1, 2)
 

time: 23.3 us -> 21.7 us (0.931)
  other arithmetic: 1.71 us -> 0.73 us
  Pallas kernels: 21.5 us -> 20.8 us
    add x1, other arithmetic: 1.71 us -> 0.73 us  [shards_kernel(): out = mixing + update.astype(jnp.float32)]
    pallas_call x1, Pallas kernels: 21.5 us -> 20.8 us  [shards_kernel(): pl.pallas_call(functools.partial(step_kernel, groups, peers, most), out_s...]
where the time goes in v4:
time: 21.7 us; the launch traced here: 21.5 us
  Pallas kernels  20.8 us (96%)
  other arithmetic  0.73 us (3%)
    pallas_call x1, Pallas kernels, shards_kernel(): pl.pallas_call(functools.partial(step_kernel, groups, peers, most), out_s...  20.8 us
    add x1, other arithmetic, shards_kernel(): out = mixing + update.astype(jnp.float32)  0.73 us

profile of v4, /device:TPU:0, one launch (start us, length us, event | category | flops | bytes accessed | tf_op | source)
XLA Modules:
  0.0 21.5 jit_solution(6011596441206694973)
XLA Ops:
  0.0 20.8 %shard_map.118 = (f32[2,256,128]{2,1,0:T(8,128)S(1)}, bf16[2,256,128]{2,1,0:T(8,128)(2,1)S(1)}) custom-call(f32[2,16,16,128]{3,2,1,0:T(8,128)} %tracers.1, f32[16,16,128]{2,1,0:T(8,128)} %layer_mass.1, f32[16,16]{1,0:T(8,128)} %courant.1, f32[128,128]{1,0:T(8,128)} %remap.1, s32[16,16]{1,0:T(8,128)} %cost_class.1, s32[1,16]{1,0:T(1,128)} %bitcast.4, ...), custom_call_target="tpu_custom_call" | custom-call | tf_op jit(solution)/shard_map/pallas_call | solution.py:442
  20.8 0.7 %convert_add_fusion = f32[2,256,128]{2,1,0:T(8,128)} fusion(f32[2,256,128]{2,1,0:T(8,128)S(1)} %get-tuple-element.7, bf16[2,256,128]{2,1,0:T(8,128)(2,1)S(1)} %get-tuple-element.8), kind=kLoop, calls=%fused_computation | loop fusion | flops 131072 | bytes 655360 | tf_op jit(solution)/shard_map/add | solution.py:493
